TPU v7x, 32 devices: a whole 2x2x4 slice. The times are simulated.
32 devices in a mesh: dp: 4 (over y, x), segment: 4 (over z), mp: 2 (over core).
Axes of the slice: x: 2, y: 2, z: 4, core: 2. Of those that a mesh axis runs over, the one named last changes fastest.
Arguments:
- trunk_in: bfloat16 [1024, 2560], P('dp', 'mp'), may hold values from -6 to 6
- norm_gain: bfloat16 [4, 2560], P('segment'), may hold values from 0.5 to 1.5
- w_gate: bfloat16 [4, 2560, 3584], P('segment', 'dp', 'mp'), may hold values from -0.125 to 0.125
- w_up: bfloat16 [4, 2560, 3584], P('segment', 'dp', 'mp'), may hold values from -0.125 to 0.125
- w_down: bfloat16 [4, 3584, 2560], P('segment', 'mp', 'dp'), may hold values from -0.09375 to 0.09375
- w_cond: bfloat16 [2560, 512], P('mp'), may hold values from -0.125 to 0.125
- w_time: bfloat16 [256, 512], replicated, may hold values from -0.375 to 0.375
- w_in: bfloat16 [70, 256], replicated, may hold values from -0.75 to 0.75
- w_mid: bfloat16 [1280, 256], replicated, may hold values from -0.15625 to 0.15625
- w_res: bfloat16 [14, 256], replicated, may hold values from -1.5 to 1.5
- w_out: bfloat16 [256, 14], replicated, may hold values from -0.375 to 0.375
- tsteps: int32 [64, 8], P('dp'), may hold values from 0 to 99
- advantage: float32 [64, 8], P('dp'), may hold values from -4 to 4
- actions: bfloat16 [64, 64, 14], P('dp'), may hold values from -6 to 6
- noise: bfloat16 [64, 8, 64, 14], P('dp'), may hold values from -6 to 6
Outputs:
- grad_w_in: float32 [70, 256], P(None, 'segment')
- grad_w_mid: float32 [1280, 256], P(None, 'segment')
- grad_w_res: float32 [14, 256], P(None, 'segment')
- grad_w_out: float32 [256, 14], P('segment')
- grad_w_time: float32 [256, 512], P(None, 'segment')
- grad_w_cond: float32 [2560, 512], P('mp', 'segment')
- grad_cond: float32 [64, 2560], P(('dp', 'segment'), 'mp')
- loss: float32 [1], replicated
All inputs are finite; a program needn't handle non-finite values.
Results may differ from a plain program's by a relative error of at most 0.035.
Values may be sent and summed in bfloat16 or wider, within the bound.
No kernel may reach another device: no remote copies, remote signals or barrier semaphores. Data moves between devices by JAX's collectives and lax.ppermute only.
A program may use at most 128 MiB of HBM per device.

v0:
```python
import math
import jax
import jax.numpy as jnp
from jax import lax
from jax.sharding import PartitionSpec as P

GROUPS = 8
TSTEPS = 100
TPS = 16
SPM = 4
SPD = 16
LEV = 8


def passed_along(block, axis, distance):
    devices = range(lax.axis_size(axis))
    route = [(i - distance, i) for i in devices if i - distance in devices]
    return lax.ppermute(block, axis, route)


def spread_2(value, axis, source):
    kept = jnp.where(lax.axis_index(axis) == source, value, 0).astype(value.dtype)
    return lax.psum(kept, axis)


def mish_value(values):
    return values * jnp.tanh(jax.nn.softplus(values))


def mish_slope(values):
    soft = jnp.tanh(jax.nn.softplus(values))
    return soft + values * jax.nn.sigmoid(values) * (1.0 - soft * soft)


def contract(form, left, right):
    return jnp.einsum(form, left, right, preferred_element_type=jnp.float32)


def alpha_table():
    grid = jnp.arange(TSTEPS + 1, dtype=jnp.float32) / TSTEPS
    curve = jnp.cos((grid + 0.008) / 1.008 * math.pi / 2.0) ** 2
    betas = jnp.minimum(1.0 - curve[1:] / curve[:-1], 0.999)
    return jnp.cumprod(1.0 - betas)


def norm_act(values):
    rows, steps, channels = values.shape
    grouped = values.reshape(rows, steps, GROUPS, channels // GROUPS)
    center = jnp.mean(grouped, axis=(1, 3), keepdims=True)
    spread = jnp.mean((grouped - center) ** 2, axis=(1, 3), keepdims=True)
    normed = (grouped - center) * lax.rsqrt(spread + 1e-05)
    return mish_value(normed.reshape(rows, steps, channels))


def columns(values):
    steps = values.shape[1]
    padded = jnp.pad(values, ((0, 0), (2, 2), (0, 0)))
    return jnp.concatenate([padded[:, tap : tap + steps] for tap in range(5)], axis=2)


def columns_adjoint(grads, width):
    total = 0.0
    for tap in range(5):
        piece = grads[:, :, tap * width : (tap + 1) * width]
        total = total + jnp.pad(piece, ((0, 0), (tap, 4 - tap), (0, 0)))
    return total[:, 2:-2]


def own_block(values, which, count, axis_number):
    width = values.shape[axis_number] // count
    return lax.dynamic_slice_in_dim(values, which * width, width, axis_number)


def denoise(
    film_cond, tsteps, advantage, actions, noise, w_in, w_mid, w_res, w_out, w_time, product
):
    row_count, levels = tsteps.shape
    horizon, action_dims = (actions.shape[1], actions.shape[2])
    channels = w_mid.shape[1]
    flat = row_count * levels
    matches = (tsteps[:, :, None] == jnp.arange(TSTEPS, dtype=jnp.int32)[None, None, :]).astype(
        jnp.float32
    )
    alpha = jnp.sum(matches * alpha_table()[None, None, :], axis=2)
    keep_root = jnp.sqrt(alpha)[:, :, None, None]
    noise_root = jnp.sqrt(1.0 - alpha)[:, :, None, None]
    noisy_act = (
        keep_root * actions.astype(jnp.float32)[:, None] + noise_root * noise.astype(jnp.float32)
    ).astype(jnp.bfloat16)
    noisy_act = noisy_act.reshape(flat, horizon, action_dims)
    half_dim = w_time.shape[0] // 2
    frequencies = jnp.exp(
        -math.log(10000.0) * jnp.arange(half_dim, dtype=jnp.float32) / (half_dim - 1)
    )
    angles = tsteps.astype(jnp.float32)[:, :, None] * frequencies[None, None, :]
    embedded = jnp.concatenate([jnp.sin(angles), jnp.cos(angles)], axis=2)
    time_act = mish_value(embedded).astype(jnp.bfloat16).reshape(flat, 2 * half_dim)
    film = film_cond[:, None, :] + product(
        "rld,dc->rlc", time_act.reshape(row_count, levels, -1), w_time
    )
    film = film.reshape(flat, 2 * channels)
    film_scale = film[:, None, :channels]
    film_shift = film[:, None, channels:]
    columns_in = columns(noisy_act)
    pre_first = product("mhk,kc->mhc", columns_in, w_in)
    act_first, first_back = jax.vjp(norm_act, pre_first)
    modulated = (film_scale * act_first + film_shift).astype(jnp.bfloat16)
    columns_mid = columns(modulated)
    pre_second = product("mhk,kc->mhc", columns_mid, w_mid)
    act_second, second_back = jax.vjp(norm_act, pre_second)
    block_out = (act_second + product("mha,ac->mhc", noisy_act, w_res)).astype(jnp.bfloat16)
    predicted = product("mhc,ca->mha", block_out, w_out)
    errors = predicted - noise.reshape(flat, horizon, action_dims).astype(jnp.float32)
    err_sum = jnp.sum(errors * errors) / (horizon * action_dims)
    weights = advantage.reshape(flat, 1, 1)
    d_pred = (2.0 * weights * errors / (horizon * action_dims)).astype(jnp.bfloat16)
    grad_out = product("mhc,mha->ca", block_out, d_pred)
    d_block = product("mha,ca->mhc", d_pred, w_out)
    grad_res = product("mha,mhc->ac", noisy_act, d_block.astype(jnp.bfloat16))
    d_second = second_back(d_block)[0].astype(jnp.bfloat16)
    grad_mid = product("mhk,mhc->kc", columns_mid, d_second)
    d_columns = product("mhc,kc->mhk", d_second, w_mid)
    d_modulated = columns_adjoint(d_columns, channels)
    d_film = jnp.concatenate(
        [jnp.sum(d_modulated * act_first, axis=1), jnp.sum(d_modulated, axis=1)], axis=1
    )
    d_first = first_back(film_scale * d_modulated)[0].astype(jnp.bfloat16)
    grad_in = product("mhk,mhc->kc", columns_in, d_first)
    grad_time = product("md,mc->dc", time_act, d_film.astype(jnp.bfloat16))
    d_film_cond = jnp.sum(d_film.reshape(row_count, levels, -1), axis=1)
    return (err_sum, grad_in, grad_mid, grad_res, grad_out, grad_time, d_film_cond)


def body(
    trunk_in,
    norm_gain,
    w_gate,
    w_up,
    w_down,
    w_cond,
    w_time,
    w_in,
    w_mid,
    w_res,
    w_out,
    tsteps,
    advantage,
    actions,
    noise,
):
    segments = lax.axis_size("segment")
    segment_index = lax.axis_index("segment")
    cores = lax.axis_size("mp")
    core_index = lax.axis_index("mp")
    gate_full, up_full, down_full = (
        lax.all_gather(w_gate, "dp", axis=1, tiled=True),
        lax.all_gather(w_up, "dp", axis=1, tiled=True),
        lax.all_gather(w_down, "dp", axis=2, tiled=True),
    )
    gate_weight = gate_full[0]
    up_weight = up_full[0]
    down_weight = down_full[0]
    norm_scale = norm_gain[0].astype(jnp.float32)
    micro_count = SPD // SPM
    batch_rows = SPM * TPS
    half_width = trunk_in.shape[1]
    inputs = trunk_in.reshape(micro_count, batch_rows, half_width)

    def trunk_layer(current):
        whole_rows = lax.all_gather(current, "mp", axis=1, tiled=True)
        widened = whole_rows.astype(jnp.float32)
        factor = lax.rsqrt(jnp.mean(widened * widened, axis=1, keepdims=True) + 1e-05)
        normed = (widened * factor * norm_scale).astype(jnp.bfloat16)
        gate_out = jnp.dot(normed, gate_weight, preferred_element_type=jnp.float32)
        up_out = jnp.dot(normed, up_weight, preferred_element_type=jnp.float32)
        hidden = (jax.nn.silu(gate_out) * up_out).astype(jnp.bfloat16)
        partial_out = jnp.dot(hidden, down_weight, preferred_element_type=jnp.float32)
        summed = lax.psum_scatter(
            partial_out.astype(jnp.bfloat16), "mp", scatter_dimension=1, tiled=True
        ).astype(jnp.float32)
        return (current.astype(jnp.float32) + summed).astype(jnp.bfloat16)

    def advance(step_index, loop_state):
        received, stored = loop_state
        fresh_rows = lax.dynamic_index_in_dim(
            inputs, jnp.minimum(step_index, micro_count - 1), 0, keepdims=False
        )
        fresh_rows = jnp.where(step_index < micro_count, fresh_rows, jnp.zeros_like(fresh_rows))
        current = jnp.where(segment_index == 0, fresh_rows, received)
        result = trunk_layer(current)
        slot_index = jnp.clip(step_index - (segments - 1), 0, micro_count - 1)
        previous = lax.dynamic_index_in_dim(stored, slot_index, 0, keepdims=False)
        kept_rows = jnp.where(step_index >= segments - 1, result, previous)
        stored = lax.dynamic_update_index_in_dim(stored, kept_rows, slot_index, 0)
        received = passed_along(result, "segment", 1)
        return (received, stored)

    start_state = (
        jnp.zeros((batch_rows, half_width), jnp.bfloat16),
        jnp.zeros((micro_count, batch_rows, half_width), jnp.bfloat16),
    )
    final_state = lax.fori_loop(0, micro_count + segments - 1, advance, start_state)
    trunk_out = final_state[1].reshape(SPD, TPS, half_width)
    cond = jnp.mean(trunk_out.astype(jnp.float32), axis=1).astype(jnp.bfloat16)
    is_last = (segment_index == segments - 1).astype(jnp.float32)
    row_total = cond.shape[0]
    own_rows = row_total // cores
    cond_act = mish_value(cond.astype(jnp.float32)).astype(jnp.bfloat16)
    film_cond = lax.psum_scatter(
        jnp.dot(cond_act, w_cond, preferred_element_type=jnp.float32).astype(jnp.bfloat16),
        "mp",
        scatter_dimension=0,
        tiled=True,
    ).astype(jnp.float32)
    begin_row = core_index * own_rows
    steps_own = lax.dynamic_slice_in_dim(tsteps, begin_row, own_rows, 0)
    advantage_own = lax.dynamic_slice_in_dim(advantage, begin_row, own_rows, 0)
    actions_own = lax.dynamic_slice_in_dim(actions, begin_row, own_rows, 0)
    noise_own = lax.dynamic_slice_in_dim(noise, begin_row, own_rows, 0)
    outcome = denoise(
        film_cond,
        steps_own,
        advantage_own,
        actions_own,
        noise_own,
        w_in,
        w_mid,
        w_res,
        w_out,
        w_time,
        contract,
    )
    err_sum, grad_in, grad_mid, grad_res, grad_out, grad_time, d_film_cond = outcome
    film_share = (d_film_cond * is_last).astype(jnp.bfloat16)
    film_all = lax.all_gather(film_share, "mp", axis=0, tiled=True)
    cond_grad_part = contract("sc,dc->sd", film_all, w_cond) * mish_slope(cond.astype(jnp.float32))
    grad_cond = lax.psum_scatter(
        cond_grad_part.astype(jnp.bfloat16), "segment", scatter_dimension=0, tiled=True
    ).astype(jnp.float32)
    local_sums = (
        lax.psum(grad_in.astype(jnp.bfloat16), ("dp", "mp")).astype(jnp.float32),
        lax.psum(grad_mid.astype(jnp.bfloat16), ("dp", "mp")).astype(jnp.float32),
        lax.psum(grad_res.astype(jnp.bfloat16), ("dp", "mp")).astype(jnp.float32),
        lax.psum(grad_out.astype(jnp.bfloat16), ("dp", "mp")).astype(jnp.float32),
        lax.psum(grad_time.astype(jnp.bfloat16), ("dp", "mp")).astype(jnp.float32),
        lax.psum(err_sum.astype(jnp.bfloat16), ("dp", "mp")).astype(jnp.float32),
    )
    act_rows, grad_rows = (
        lax.all_gather(cond_act, "dp", axis=0, tiled=True),
        lax.all_gather(film_all, "dp", axis=0, tiled=True),
    )
    local_cond = contract("sd,sc->dc", act_rows, grad_rows)
    fanned = (
        spread_2(local_sums[0].astype(jnp.bfloat16), "segment", segments - 1).astype(jnp.float32),
        spread_2(local_sums[1].astype(jnp.bfloat16), "segment", segments - 1).astype(jnp.float32),
        spread_2(local_sums[2].astype(jnp.bfloat16), "segment", segments - 1).astype(jnp.float32),
        spread_2(local_sums[3].astype(jnp.bfloat16), "segment", segments - 1).astype(jnp.float32),
        spread_2(local_sums[4].astype(jnp.bfloat16), "segment", segments - 1).astype(jnp.float32),
        spread_2(local_sums[5].astype(jnp.bfloat16), "segment", segments - 1).astype(jnp.float32),
        spread_2(local_cond.astype(jnp.bfloat16), "segment", segments - 1).astype(local_cond.dtype),
    )
    summed_grads = fanned[:6]
    grad_w_cond = own_block(fanned[6], segment_index, segments, 1)
    replicas = lax.axis_size("dp")
    loss = (summed_grads[5] / (replicas * SPD * LEV)).reshape(1)
    return (
        own_block(summed_grads[0], segment_index, segments, 1),
        own_block(summed_grads[1], segment_index, segments, 1),
        own_block(summed_grads[2], segment_index, segments, 1),
        own_block(summed_grads[3], segment_index, segments, 0),
        own_block(summed_grads[4], segment_index, segments, 1),
        grad_w_cond,
        grad_cond,
        loss,
    )


def solution(mesh):
    in_specs = (
        P("dp", "mp"),
        P("segment", None),
        P("segment", "dp", "mp"),
        P("segment", "dp", "mp"),
        P("segment", "mp", "dp"),
        P("mp", None),
        P(),
        P(),
        P(),
        P(),
        P(),
        P("dp", None),
        P("dp", None),
        P("dp", None, None),
        P("dp", None, None, None),
    )
    out_specs = (
        P(None, "segment"),
        P(None, "segment"),
        P(None, "segment"),
        P("segment", None),
        P(None, "segment"),
        P("mp", "segment"),
        P(("dp", "segment"), "mp"),
        P(),
    )
    return jax.shard_map(body, mesh=mesh, in_specs=in_specs, out_specs=out_specs, check_vma=False)
```

profile of v0, /device:TPU:0, one launch (start us, length us, event | category | flops | bytes accessed | tf_op | source)
XLA Modules:
  0.0 852.6 jit_solution(11993340985135364638)
XLA Ops:
  14.4 6.5 concatenate.15
  20.9 4.2 fusion.91
  31.5 75.1 %all-gather.4.cloned.1.call-done = bf16[1,2560,1792]{2,1,0:T(8,128)(2,1)} async-done(((bf16[1,640,1792]{2,1,0:T(8,128)(2,1)}), bf16[1,2560,1792]{2,1,0:T(8,128)(2,1)}) %all-gather.4.cloned.1.call-update) | async-done | bytes 9175056 | tf_op jit(solution)/shard_map/all_gather | solution.py:156
  106.6 95.9 %all-gather.6.cloned.1.call-done = bf16[1,2560,1792]{2,1,0:T(8,128)(2,1)} async-done(((bf16[1,640,1792]{2,1,0:T(8,128)(2,1)}), bf16[1,2560,1792]{2,1,0:T(8,128)(2,1)}) %all-gather.6.cloned.1.call-update) | async-done | bytes 9175056 | tf_op jit(solution)/shard_map/all_gather | solution.py:157
  202.5 95.9 %all-gather.8.cloned.1.call-done = bf16[1,1792,2560]{2,1,0:T(8,128)(2,1)} async-done(((bf16[1,1792,640]{2,1,0:T(8,128)(2,1)}), bf16[1,1792,2560]{2,1,0:T(8,128)(2,1)}) %all-gather.8.cloned.1.call-update) | async-done | bytes 9175056 | tf_op jit(solution)/shard_map/all_gather | solution.py:158
  299.3 263.3 %while.17 = (s32[]{:T(128)}, bf16[64,1280]{1,0:T(8,128)(2,1)S(1)}, bf16[4,64,1280]{2,1,0:T(8,128)(2,1)}, pred[]{:T(512)}, bf16[4,64,1280]{2,1,0:T(8,128)(2,1)}, ...) while((s32[]{:T(128)}, bf16[64,1280]{1,0:T(8,128)(2,1)S(1)}, ...), condition=%wide.region_5.6_spmd, body=%wide.region_2.5_spmd.sunk | while | flops 1764835328 | bytes 34035272 | solution.py:202
  302.5 5.4 fusion.126
  307.9 10.3 %convolution_convert_fusion.5 = bf16[64,2560]{1,0:T(8,128)(2,1)} fusion(bf16[1792,2560]{1,0:T(8,128)(2,1)} %get-tuple-element.408, bf16[2560,1792]{1,0:T(8,128)(2,1)} %get-tuple-element.407, f32[64,1792]{1,0:T(8,128)S(1)} %fusion.126, bf16[64,2560]{1,0:T(8,128)(2,1)S(1)} %all_gather.35, f32[2560]{0:T(1024)S(1)} %get-tuple-element.405, ...), kind=kOutput, calls=%fused_computation.clone.1 | convolution fusion | flops 1175912448 | bytes 19474688 | tf_op jit(solution)/shard_map/while/body/eval_jaxpr/dot_general | solution.py:177
  319.2 7.0 reduce-scatter.5.cloned.1.call-done
  331.4 4.0 collective-permute-done
  338.5 5.4 fusion.126
  343.9 10.3 %convolution_convert_fusion.5 = bf16[64,2560]{1,0:T(8,128)(2,1)} fusion(bf16[1792,2560]{1,0:T(8,128)(2,1)} %get-tuple-element.408, bf16[2560,1792]{1,0:T(8,128)(2,1)} %get-tuple-element.407, f32[64,1792]{1,0:T(8,128)S(1)} %fusion.126, bf16[64,2560]{1,0:T(8,128)(2,1)S(1)} %all_gather.35, f32[2560]{0:T(1024)S(1)} %get-tuple-element.405, ...), kind=kOutput, calls=%fused_computation.clone.1 | convolution fusion | flops 1175912448 | bytes 19474688 | tf_op jit(solution)/shard_map/while/body/eval_jaxpr/dot_general | solution.py:177
  355.1 8.9 %reduce-scatter.5.cloned.1.call-done = bf16[64,1280]{1,0:T(8,128)(2,1)} async-done(((bf16[64,2560]{1,0:T(8,128)(2,1)}), bf16[64,1280]{1,0:T(8,128)(2,1)}) %reduce-scatter.5.cloned.1.call-update) | async-done | bytes 163856 | tf_op jit(solution)/shard_map/while/body/eval_jaxpr/reduce_scatter | solution.py:178
  369.3 3.9 collective-permute-done
  376.4 5.4 fusion.126
  381.8 10.3 %convolution_convert_fusion.5 = bf16[64,2560]{1,0:T(8,128)(2,1)} fusion(bf16[1792,2560]{1,0:T(8,128)(2,1)} %get-tuple-element.408, bf16[2560,1792]{1,0:T(8,128)(2,1)} %get-tuple-element.407, f32[64,1792]{1,0:T(8,128)S(1)} %fusion.126, bf16[64,2560]{1,0:T(8,128)(2,1)S(1)} %all_gather.35, f32[2560]{0:T(1024)S(1)} %get-tuple-element.405, ...), kind=kOutput, calls=%fused_computation.clone.1 | convolution fusion | flops 1175912448 | bytes 19474688 | tf_op jit(solution)/shard_map/while/body/eval_jaxpr/dot_general | solution.py:177
  393.0 8.9 %reduce-scatter.5.cloned.1.call-done = bf16[64,1280]{1,0:T(8,128)(2,1)} async-done(((bf16[64,2560]{1,0:T(8,128)(2,1)}), bf16[64,1280]{1,0:T(8,128)(2,1)}) %reduce-scatter.5.cloned.1.call-update) | async-done | bytes 163856 | tf_op jit(solution)/shard_map/while/body/eval_jaxpr/reduce_scatter | solution.py:178
  407.2 3.9 collective-permute-done
  414.3 5.4 fusion.126
  419.7 10.3 %convolution_convert_fusion.5 = bf16[64,2560]{1,0:T(8,128)(2,1)} fusion(bf16[1792,2560]{1,0:T(8,128)(2,1)} %get-tuple-element.408, bf16[2560,1792]{1,0:T(8,128)(2,1)} %get-tuple-element.407, f32[64,1792]{1,0:T(8,128)S(1)} %fusion.126, bf16[64,2560]{1,0:T(8,128)(2,1)S(1)} %all_gather.35, f32[2560]{0:T(1024)S(1)} %get-tuple-element.405, ...), kind=kOutput, calls=%fused_computation.clone.1 | convolution fusion | flops 1175912448 | bytes 19474688 | tf_op jit(solution)/shard_map/while/body/eval_jaxpr/dot_general | solution.py:177
  430.9 8.9 %reduce-scatter.5.cloned.1.call-done = bf16[64,1280]{1,0:T(8,128)(2,1)} async-done(((bf16[64,2560]{1,0:T(8,128)(2,1)}), bf16[64,1280]{1,0:T(8,128)(2,1)}) %reduce-scatter.5.cloned.1.call-update) | async-done | bytes 163856 | tf_op jit(solution)/shard_map/while/body/eval_jaxpr/reduce_scatter | solution.py:178
  445.1 3.9 collective-permute-done
  452.2 5.4 fusion.126
  457.5 10.3 %convolution_convert_fusion.5 = bf16[64,2560]{1,0:T(8,128)(2,1)} fusion(bf16[1792,2560]{1,0:T(8,128)(2,1)} %get-tuple-element.408, bf16[2560,1792]{1,0:T(8,128)(2,1)} %get-tuple-element.407, f32[64,1792]{1,0:T(8,128)S(1)} %fusion.126, bf16[64,2560]{1,0:T(8,128)(2,1)S(1)} %all_gather.35, f32[2560]{0:T(1024)S(1)} %get-tuple-element.405, ...), kind=kOutput, calls=%fused_computation.clone.1 | convolution fusion | flops 1175912448 | bytes 19474688 | tf_op jit(solution)/shard_map/while/body/eval_jaxpr/dot_general | solution.py:177
  468.8 8.9 %reduce-scatter.5.cloned.1.call-done = bf16[64,1280]{1,0:T(8,128)(2,1)} async-done(((bf16[64,2560]{1,0:T(8,128)(2,1)}), bf16[64,1280]{1,0:T(8,128)(2,1)}) %reduce-scatter.5.cloned.1.call-update) | async-done | bytes 163856 | tf_op jit(solution)/shard_map/while/body/eval_jaxpr/reduce_scatter | solution.py:178
  483.0 3.9 collective-permute-done
  490.0 5.4 fusion.126
  495.4 10.3 %convolution_convert_fusion.5 = bf16[64,2560]{1,0:T(8,128)(2,1)} fusion(bf16[1792,2560]{1,0:T(8,128)(2,1)} %get-tuple-element.408, bf16[2560,1792]{1,0:T(8,128)(2,1)} %get-tuple-element.407, f32[64,1792]{1,0:T(8,128)S(1)} %fusion.126, bf16[64,2560]{1,0:T(8,128)(2,1)S(1)} %all_gather.35, f32[2560]{0:T(1024)S(1)} %get-tuple-element.405, ...), kind=kOutput, calls=%fused_computation.clone.1 | convolution fusion | flops 1175912448 | bytes 19474688 | tf_op jit(solution)/shard_map/while/body/eval_jaxpr/dot_general | solution.py:177
  506.7 8.9 %reduce-scatter.5.cloned.1.call-done = bf16[64,1280]{1,0:T(8,128)(2,1)} async-done(((bf16[64,2560]{1,0:T(8,128)(2,1)}), bf16[64,1280]{1,0:T(8,128)(2,1)}) %reduce-scatter.5.cloned.1.call-update) | async-done | bytes 163856 | tf_op jit(solution)/shard_map/while/body/eval_jaxpr/reduce_scatter | solution.py:178
  527.9 5.4 fusion.126
  533.3 10.3 %convolution_convert_fusion.5 = bf16[64,2560]{1,0:T(8,128)(2,1)} fusion(bf16[1792,2560]{1,0:T(8,128)(2,1)} %get-tuple-element.408, bf16[2560,1792]{1,0:T(8,128)(2,1)} %get-tuple-element.407, f32[64,1792]{1,0:T(8,128)S(1)} %fusion.126, bf16[64,2560]{1,0:T(8,128)(2,1)S(1)} %all_gather.35, f32[2560]{0:T(1024)S(1)} %get-tuple-element.405, ...), kind=kOutput, calls=%fused_computation.clone.1 | convolution fusion | flops 1175912448 | bytes 19474688 | tf_op jit(solution)/shard_map/while/body/eval_jaxpr/dot_general | solution.py:177
  544.6 8.9 %reduce-scatter.5.cloned.1.call-done = bf16[64,1280]{1,0:T(8,128)(2,1)} async-done(((bf16[64,2560]{1,0:T(8,128)(2,1)}), bf16[64,1280]{1,0:T(8,128)(2,1)}) %reduce-scatter.5.cloned.1.call-update) | async-done | bytes 163856 | tf_op jit(solution)/shard_map/while/body/eval_jaxpr/reduce_scatter | solution.py:178
  570.3 9.4 %all_gather.31 = bf16[64,1280]{1,0:T(8,128)(2,1)} all-gather(bf16[16,1280]{1,0:T(8,128)(2,1)S(1)} %fusion.57), channel_id=1, replica_groups=mesh['dp'=4,'segment'=4,'mp'=2] {'dp'}, dimensions={0}, use_global_device_ids=true | all-gather | bytes 204800 | tf_op jit(solution)/shard_map/all_gather | solution.py:249
  581.6 4.7 add_convert_fusion.3
  594.1 5.3 fusion.92
  603.0 5.2 fusion.28
  610.4 7.9 multiply_reduce_fusion.8
  622.2 5.0 add_convert_fusion.2
  627.3 7.8 fusion.30
  635.1 8.6 %fusion.45 = f32[64,64,1280]{2,1,0:T(8,128)} fusion(bf16[64,64,256]{2,1,0:T(8,128)(2,1)S(1)} %add_convert_fusion.2, bf16[1280,256]{1,0:T(8,128)(2,1)S(1)} %copy-done.12), kind=kOutput, calls=%fused_computation.87 | convolution fusion | flops 2684354560 | bytes 23724032 | tf_op jit(solution)/shard_map/mhc,kc->mhk/dot_general | solution.py:36
  643.7 12.7 %fusion.88 = (f32[64,64,256]{2,1,0:T(8,128)S(1)}, f32[64,64,256]{2,1,0:T(8,128)S(1)}, f32[64,64,256]{2,1,0:T(8,128)}, f32[64,64,256]{2,1,0:T(8,128)}, f32[64,64,256]{2,1,0:T(8,128)}) fusion(f32[64,64,1280]{2,1,0:T(8,128)} %fusion.45), kind=kLoop, calls=%fused_computation.189 | loop fusion | bytes 41943040 | tf_op jit(solution)/shard_map/slice | solution.py:64
  656.4 13.4 %multiply_reduce_fusion = (f32[64,256]{1,0:T(8,128)S(1)}, f32[64,256]{1,0:T(8,128)S(1)}, f32[64,256]{1,0:T(8,128)}, f32[64,256]{1,0:T(8,128)S(1)}, f32[64,64,256]{2,1,0:T(8,128)}) fusion(f32[64,256]{1,0:T(8,128)S(1)} %copy.102, f32[64,64,256]{2,1,0:T(8,128)S(1)} %copy-done.2, f32[64,256]{1,0:T(8,128)S(1)} %copy.100, f32[64,256]{1,0:T(8,128)S(1)} %copy-done.8, ...), kind=kLoop, calls=%fused_computation.42 | loop fusion | flops 35586048 | bytes 29818880 | tf_op jit(solution)/shard_map/reduce_sum | solution.py:125
  671.8 8.4 all_gather.33
  693.8 49.4 %all-reduce.16.cloned.1.call-done = (bf16[1280,256]{0,1:T(8,128)(2,1)}, bf16[256,512]{1,0:T(8,128)(2,1)}) async-done(((bf16[1280,256]{0,1:T(8,128)(2,1)}, bf16[256,512]{1,0:T(8,128)(2,1)}), (bf16[1280,256]{0,1:T(8,128)(2,1)}, bf16[256,512]{1,0:T(8,128)(2,1)})) %all-reduce.16.cloned.1.call-update) | async-done | bytes 917520 | tf_op jit(solution)/shard_map/psum | solution.py:242
  745.6 4.8 fusion.37
  750.4 24.5 %all-reduce.8 = (bf16[70,256]{0,1:T(8,128)(2,1)S(1)}, bf16[14,256]{1,0:T(8,128)(2,1)S(1)}, bf16[256,14]{0,1:T(8,128)(2,1)S(1)}, bf16[]{:T(256)}) all-reduce(bf16[70,256]{0,1:T(8,128)(2,1)S(1)} %fusion.37, bf16[14,256]{1,0:T(8,128)(2,1)S(1)} %copy-done.25, ...), channel_id=1, replica_groups=mesh['dp'=4,'segment'=4,'mp'=2] {'dp','mp'}, use_global_device_ids=true, to_apply=%region_28.30 | all-reduce | flops 25089 | bytes 100356 | tf_op jit(solution)/shard_map/psum | solution.py:241
  776.1 26.0 %all-reduce.19 = (bf16[70,256]{0,1:T(8,128)(2,1)S(1)}, bf16[14,256]{1,0:T(8,128)(2,1)S(1)}, bf16[256,14]{0,1:T(8,128)(2,1)S(1)}, bf16[16,1280]{1,0:T(8,128)(2,1)S(1)}, bf16[]{:T(256)}) all-reduce(bf16[70,256]{0,1:T(8,128)(2,1)S(1)} %broadcast_select_fusion.2, ...), channel_id=1, replica_groups=mesh['dp'=4,'segment'=4,'mp'=2] {'segment'}, use_global_device_ids=true, to_apply=%region_29.31 | all-reduce | flops 45569 | bytes 182276 | tf_op jit(solution)/shard_map/psum | solution.py:23
  805.3 34.1 %all-reduce.18.cloned.1.call-done = (bf16[1280,256]{0,1:T(8,128)(2,1)}, bf16[256,512]{1,0:T(8,128)(2,1)}, bf16[1280,512]{1,0:T(8,128)(2,1)}) async-done(((bf16[1280,256]{0,1:T(8,128)(2,1)}, bf16[256,512]{1,0:T(8,128)(2,1)}, bf16[1280,512]{1,0:T(8,128)(2,1)}), (bf16[1280,256]{0,1:T(8,128)(2,1)}, bf16[256,512]{1,0:T(8,128)(2,1)}, bf16[1280,512]{1,0:T(8,128)(2,1)})) %all-reduce.18.cloned.1.call-update) | async-done | bytes 2228240 | tf_op jit(solution)/shard_map/psum | solution.py:23
  (249 shorter events, 138.9 us)
Async XLA Ops:
  7.2 556.9 %copy-start = (bf16[1280,512]{1,0:T(8,128)(2,1)S(1)}, bf16[1280,512]{1,0:T(8,128)(2,1)}, u32[]{:S(2)}) copy-start(bf16[1280,512]{1,0:T(8,128)(2,1)} %param.23) | copy-start | bytes 3932164
  7.2 2.8 copy-start.26
  7.2 3.3 copy-start.15
  7.2 99.4 %all-gather.4.cloned.1.call-start = ((), (), s32[]{:S(2)}) async-start(), calls=%async_computation.2 | async-start | bytes 11468800 | tf_op jit(solution)/shard_map/all_gather | solution.py:156
  7.9 194.6 %all-gather.6.cloned.1.call-start = ((), (), s32[]{:S(2)}) async-start(), calls=%async_computation.3 | async-start | bytes 11468800 | tf_op jit(solution)/shard_map/all_gather | solution.py:157
  8.7 289.7 %all-gather.8.cloned.1.call-start = ((), (), s32[]{:S(2)}) async-start(), calls=%async_computation.4 | async-start | bytes 11468800 | tf_op jit(solution)/shard_map/all_gather | solution.py:158
  11.2 591.8 %copy-start.4 = (bf16[8,8,64,14]{3,2,1,0:T(8,128)(2,1)}, bf16[8,8,64,14]{3,2,1,0:T(8,128)(2,1)S(1)}, u32[]{:S(2)}) copy-start(bf16[8,8,64,14]{3,2,1,0:T(8,128)(2,1)S(1)} %copy.96) | copy-start | bytes 344068
  14.4 6.5 copy-start.24
  20.8 7.6 copy-start.27
  299.3 26.8 %reduce-scatter.5.cloned.1.call-start = ((), (), s32[]{:S(2)}) async-start(), calls=%async_computation.8 | async-start | bytes 491520 | tf_op jit(solution)/shard_map/while/body/eval_jaxpr/reduce_scatter | solution.py:178
  327.8 7.6 collective-permute-start
  335.3 28.7 %reduce-scatter.5.cloned.1.call-start = ((), (), s32[]{:S(2)}) async-start(), calls=%async_computation.8 | async-start | bytes 491520 | tf_op jit(solution)/shard_map/while/body/eval_jaxpr/reduce_scatter | solution.py:178
  365.7 7.5 collective-permute-start
  373.2 28.7 %reduce-scatter.5.cloned.1.call-start = ((), (), s32[]{:S(2)}) async-start(), calls=%async_computation.8 | async-start | bytes 491520 | tf_op jit(solution)/shard_map/while/body/eval_jaxpr/reduce_scatter | solution.py:178
  403.6 7.5 collective-permute-start
  411.1 28.7 %reduce-scatter.5.cloned.1.call-start = ((), (), s32[]{:S(2)}) async-start(), calls=%async_computation.8 | async-start | bytes 491520 | tf_op jit(solution)/shard_map/while/body/eval_jaxpr/reduce_scatter | solution.py:178
  441.5 7.5 collective-permute-start
  449.0 28.7 %reduce-scatter.5.cloned.1.call-start = ((), (), s32[]{:S(2)}) async-start(), calls=%async_computation.8 | async-start | bytes 491520 | tf_op jit(solution)/shard_map/while/body/eval_jaxpr/reduce_scatter | solution.py:178
  479.4 7.5 collective-permute-start
  486.9 28.7 %reduce-scatter.5.cloned.1.call-start = ((), (), s32[]{:S(2)}) async-start(), calls=%async_computation.8 | async-start | bytes 491520 | tf_op jit(solution)/shard_map/while/body/eval_jaxpr/reduce_scatter | solution.py:178
  517.2 7.5 collective-permute-start
  524.8 28.7 %reduce-scatter.5.cloned.1.call-start = ((), (), s32[]{:S(2)}) async-start(), calls=%async_computation.8 | async-start | bytes 491520 | tf_op jit(solution)/shard_map/while/body/eval_jaxpr/reduce_scatter | solution.py:178
  555.1 7.5 collective-permute-start
  562.7 17.0 %reduce-scatter.3.cloned.1.call-start = ((), (), s32[]{:S(2)}) async-start(), calls=%async_computation.5 | async-start | bytes 24576 | tf_op jit(solution)/shard_map/reduce_scatter | solution.py:209
  564.0 16.4 %copy-start.9 = (f32[16,1280]{1,0:T(8,128)}, f32[16,1280]{1,0:T(8,128)S(1)}, u32[]{:S(2)}) copy-start(f32[16,1280]{1,0:T(8,128)S(1)} %convert_reduce_fusion) | copy-start | bytes 245764
  565.0 178.2 %all-reduce.16.cloned.1.call-start = ((), (), s32[]{:S(2)}) async-start(), calls=%async_computation.6 | async-start | bytes 1835008 | tf_op jit(solution)/shard_map/psum | solution.py:242
  581.6 6.7 copy-start.7
  591.7 2.3 copy-start.11
  594.1 5.3 copy-start.16
  599.4 3.5 copy-start.31
  602.9 5.2 copy-start.17
  603.0 5.2 copy-start.28
  603.0 6.8 copy-start.30
  627.3 7.8 copy-start.12
  643.7 12.7 %copy-start.2 = (f32[64,64,256]{2,1,0:T(8,128)S(1)}, f32[64,64,256]{2,1,0:T(8,128)}, u32[]{:S(2)}) copy-start(f32[64,64,256]{2,1,0:T(8,128)} %get-tuple-element.301) | copy-start | bytes 12582916
  643.7 12.7 %copy-start.8 = (f32[64,256]{1,0:T(8,128)S(1)}, f32[64,256]{1,0:T(8,128)}, u32[]{:S(2)}) copy-start(f32[64,256]{1,0:T(8,128)} %copy-done.7) | copy-start | bytes 196612
  669.8 15.0 %copy-start.22 = (f32[64,128]{1,0:T(8,128)S(1)}, f32[64,128]{1,0:T(8,128)}, u32[]{:S(2)}) copy-start(f32[64,128]{1,0:T(8,128)} %get-tuple-element.298) | copy-start | bytes 98308
  669.8 15.0 %copy-start.23 = (f32[64,128]{1,0:T(8,128)S(1)}, f32[64,128]{1,0:T(8,128)}, u32[]{:S(2)}) copy-start(f32[64,128]{1,0:T(8,128)} %get-tuple-element.299) | copy-start | bytes 98308
  669.8 16.0 %copy-start.19 = (bf16[64,1280]{1,0:T(8,128)(2,1)S(1)}, bf16[64,1280]{1,0:T(8,128)(2,1)}, u32[]{:S(2)}) copy-start(bf16[64,1280]{1,0:T(8,128)(2,1)} %all_gather.31) | copy-start | bytes 491524
  671.8 14.0 %copy-start.20 = (bf16[16,512]{1,0:T(8,128)(2,1)}, bf16[16,512]{1,0:T(8,128)(2,1)S(1)}, u32[]{:S(2)}) copy-start(bf16[16,512]{1,0:T(8,128)(2,1)S(1)} %all_gather.32) | copy-start | bytes 49156
  680.5 5.3 copy-start.13
  680.6 10.5 %copy-start.5 = (bf16[8,8,64,14]{3,2,1,0:T(8,128)(2,1)S(1)}, bf16[8,8,64,14]{3,2,1,0:T(8,128)(2,1)}, u32[]{:S(2)}) copy-start(bf16[8,8,64,14]{3,2,1,0:T(8,128)(2,1)} %copy-done.4) | copy-start | bytes 344068
  685.8 153.6 %all-reduce.18.cloned.1.call-start = ((), (), s32[]{:S(2)}) async-start(), calls=%async_computation.7 | async-start | bytes 4456448 | tf_op jit(solution)/shard_map/psum | solution.py:23
  687.5 58.1 %copy-start.6 = (bf16[64,64,70]{2,1,0:T(8,128)(2,1)S(1)}, bf16[64,64,70]{2,1,0:T(8,128)(2,1)}, u32[]{:S(2)}) copy-start(bf16[64,64,70]{2,1,0:T(8,128)(2,1)} %concatenate.15) | copy-start | bytes 1720324
  693.8 51.8 %copy-start.14 = (f32[64,256]{1,0:T(8,128)S(1)}, f32[64,256]{1,0:T(8,128)}, u32[]{:S(2)}) copy-start(f32[64,256]{1,0:T(8,128)} %copy-done.13) | copy-start | bytes 196612
  745.6 4.8 copy-start.25
  745.6 30.0 %copy-start.10 = (f32[16,1280]{1,0:T(8,128)S(1)}, f32[16,1280]{1,0:T(8,128)}, u32[]{:S(2)}) copy-start(f32[16,1280]{1,0:T(8,128)} %copy-done.9) | copy-start | bytes 245764
  745.6 30.0 %copy-start.21 = (bf16[16,512]{1,0:T(8,128)(2,1)S(1)}, bf16[16,512]{1,0:T(8,128)(2,1)}, u32[]{:S(2)}) copy-start(bf16[16,512]{1,0:T(8,128)(2,1)} %copy-done.20) | copy-start | bytes 49156
  (4 other events, 8.8 us)
Sparse Core Ops, SparseCore 0:
  9.9 96.7 all-gather.3
  108.5 94.0 all-gather.5
  204.4 94.0 all-gather.7
  318.3 7.7 reduce-scatter.4
  354.3 9.6 reduce-scatter.4
  392.2 9.6 reduce-scatter.4
  430.1 9.6 reduce-scatter.4
  468.0 9.6 reduce-scatter.4
  505.9 9.6 reduce-scatter.4
  543.8 9.6 reduce-scatter.4
  566.2 9.4 reduce-scatter.2
  685.9 57.1 all-reduce.15
  746.3 93.0 all-reduce.17
where the time goes:
time: 862 us; the launch traced here: 853 us
  waiting for transfers between devices  440 us (51%)
  matrix products  163 us (19%)
  blocking collectives  84.6 us (10%)
  other arithmetic  76.7 us (9%)
  local copies, waits for them, and re-layouts  42.8 us (5%)
  starting transfers between devices  25.4 us (3%)
  between operations  18.9 us (2%)
    all_gather x1, waiting for transfers between devices, body(): lax.all_gather(w_down, 'dp', axis=2, tiled=True)  95.9 us
    all_gather x1, waiting for transfers between devices, body(): lax.all_gather(w_up, 'dp', axis=1, tiled=True)  95.9 us
    all_gather x1, waiting for transfers between devices, body(): lax.all_gather(w_gate, 'dp', axis=1, tiled=True)  75.1 us
    dot_general x7, matrix products, trunk_layer(): jnp.dot(hidden, down_weight, preferred_element_type=jnp.float32)  72.1 us
    reduce_scatter x7, waiting for transfers between devices, trunk_layer(): lax.psum_scatter(partial_out.astype(jnp.bfloat16), 'mp', scatter_dimensio...  60.3 us
    dot_general x14, matrix products, contract(): return jnp.einsum(form, left, right, preferred_element_type=jnp.float32)  52.7 us
    psum x1, waiting for transfers between devices, body(): lax.psum(grad_mid.astype(jnp.bfloat16), ('dp', 'mp')).astype(jnp.float32)  49.4 us
    dot_general x7, matrix products, trunk_layer(): gate_out = jnp.dot(normed, gate_weight, preferred_element_type=jnp.float32)  37.6 us
  transfers between devices with their start and end apart: 20, of which 19 were waited for; matrix products, arithmetic and copies ran while one was open for 6% of the time, Pallas kernels for 0%

commit v1 on v0

--- a/solution.py
+++ b/solution.py
@@ -1,3 +1,4 @@
+import functools
 import math
 import jax
 import jax.numpy as jnp
@@ -10,6 +11,14 @@
 SPM = 4
 SPD = 16
 LEV = 8
+
+
+def _play_area(a0, axis_id, named_axis):
+    outcome_arr = jax.lax.psum(a0, axis_id)
+    return jax.lax.psum(outcome_arr, named_axis)
+
+
+order_orders_on_mesh = functools.partial(_play_area, axis_id="mp", named_axis="dp")
 
 
 def passed_along(block, axis, distance):
@@ -239,7 +248,7 @@
     ).astype(jnp.float32)
     local_sums = (
         lax.psum(grad_in.astype(jnp.bfloat16), ("dp", "mp")).astype(jnp.float32),
-        lax.psum(grad_mid.astype(jnp.bfloat16), ("dp", "mp")).astype(jnp.float32),
+        order_orders_on_mesh(grad_mid.astype(jnp.bfloat16)).astype(jnp.float32),
         lax.psum(grad_res.astype(jnp.bfloat16), ("dp", "mp")).astype(jnp.float32),
         lax.psum(grad_out.astype(jnp.bfloat16), ("dp", "mp")).astype(jnp.float32),
         lax.psum(grad_time.astype(jnp.bfloat16), ("dp", "mp")).astype(jnp.float32),

time: 862 us -> 914 us (1.060)
  waiting for transfers between devices: 440 us -> 490 us
    psum x1 -> x3, waiting for transfers between devices: 49.4 us -> 97.1 us  [the longest x1 48.8 us: body(): lax.psum(grad_time.astype(jnp.bfloat16), ('dp', 'mp')).astype(jnp.float32)]
  transfers between devices with their start and end apart: 20 -> 22, of which waited for: 19 -> 20; matrix products, arithmetic and copies ran while one was open for 6% -> 9% of each run, Pallas kernels for 0% -> 0%
where the time goes in v1:
time: 914 us; the launch traced here: 905 us
  waiting for transfers between devices  490 us (54%)
  matrix products  167 us (18%)
  blocking collectives  84.3 us (9%)
  other arithmetic  75.9 us (8%)
  local copies, waits for them, and re-layouts  43 us (5%)
  starting transfers between devices  25.5 us (3%)
  between operations  19 us (2%)
    all_gather x1, waiting for transfers between devices, body(): lax.all_gather(w_down, 'dp', axis=2, tiled=True)  95.9 us
    all_gather x1, waiting for transfers between devices, body(): lax.all_gather(w_up, 'dp', axis=1, tiled=True)  95.9 us
    all_gather x1, waiting for transfers between devices, body(): lax.all_gather(w_gate, 'dp', axis=1, tiled=True)  75.1 us
    dot_general x7, matrix products, trunk_layer(): jnp.dot(hidden, down_weight, preferred_element_type=jnp.float32)  72.1 us
    reduce_scatter x7, waiting for transfers between devices, trunk_layer(): lax.psum_scatter(partial_out.astype(jnp.bfloat16), 'mp', scatter_dimensio...  60.3 us
    dot_general x14, matrix products, contract(): return jnp.einsum(form, left, right, preferred_element_type=jnp.float32)  56.3 us
    psum x1, waiting for transfers between devices, body(): lax.psum(grad_time.astype(jnp.bfloat16), ('dp', 'mp')).astype(jnp.float32)  48.8 us
    psum x1, waiting for transfers between devices, _play_area(): return jax.lax.psum(outcome_arr, named_axis)  48.3 us
  transfers between devices with their start and end apart: 22, of which 20 were waited for; matrix products, arithmetic and copies ran while one was open for 9% of the time, Pallas kernels for 0%

profile of v1, /device:TPU:0, one launch (start us, length us, event | category | flops | bytes accessed | tf_op | source)
XLA Modules:
  0.0 904.7 jit_solution(7498700012790003516)
XLA Ops:
  14.4 6.5 concatenate.15
  20.9 4.2 fusion.91
  31.5 75.1 %all-gather.4.cloned.1.call-done = bf16[1,2560,1792]{2,1,0:T(8,128)(2,1)} async-done(((bf16[1,640,1792]{2,1,0:T(8,128)(2,1)}), bf16[1,2560,1792]{2,1,0:T(8,128)(2,1)}) %all-gather.4.cloned.1.call-update) | async-done | bytes 9175056 | tf_op jit(solution)/shard_map/all_gather | solution.py:165
  106.6 95.9 %all-gather.6.cloned.1.call-done = bf16[1,2560,1792]{2,1,0:T(8,128)(2,1)} async-done(((bf16[1,640,1792]{2,1,0:T(8,128)(2,1)}), bf16[1,2560,1792]{2,1,0:T(8,128)(2,1)}) %all-gather.6.cloned.1.call-update) | async-done | bytes 9175056 | tf_op jit(solution)/shard_map/all_gather | solution.py:166
  202.5 95.9 %all-gather.8.cloned.1.call-done = bf16[1,1792,2560]{2,1,0:T(8,128)(2,1)} async-done(((bf16[1,1792,640]{2,1,0:T(8,128)(2,1)}), bf16[1,1792,2560]{2,1,0:T(8,128)(2,1)}) %all-gather.8.cloned.1.call-update) | async-done | bytes 9175056 | tf_op jit(solution)/shard_map/all_gather | solution.py:167
  299.3 263.3 %while.17 = (s32[]{:T(128)}, bf16[64,1280]{1,0:T(8,128)(2,1)S(1)}, bf16[4,64,1280]{2,1,0:T(8,128)(2,1)}, pred[]{:T(512)}, bf16[4,64,1280]{2,1,0:T(8,128)(2,1)}, ...) while((s32[]{:T(128)}, bf16[64,1280]{1,0:T(8,128)(2,1)S(1)}, ...), condition=%wide.region_5.6_spmd, body=%wide.region_2.5_spmd.sunk | while | flops 1764835328 | bytes 34035272 | solution.py:211
  302.5 5.4 fusion.126
  307.9 10.3 %convolution_convert_fusion.5 = bf16[64,2560]{1,0:T(8,128)(2,1)} fusion(bf16[1792,2560]{1,0:T(8,128)(2,1)} %get-tuple-element.406, bf16[2560,1792]{1,0:T(8,128)(2,1)} %get-tuple-element.405, f32[64,1792]{1,0:T(8,128)S(1)} %fusion.126, bf16[64,2560]{1,0:T(8,128)(2,1)S(1)} %all_gather.35, f32[2560]{0:T(1024)S(1)} %get-tuple-element.403, ...), kind=kOutput, calls=%fused_computation.clone.1 | convolution fusion | flops 1175912448 | bytes 19474688 | tf_op jit(solution)/shard_map/while/body/eval_jaxpr/dot_general | solution.py:186
  319.2 7.0 reduce-scatter.5.cloned.1.call-done
  331.4 4.0 collective-permute-done
  338.5 5.4 fusion.126
  343.9 10.3 %convolution_convert_fusion.5 = bf16[64,2560]{1,0:T(8,128)(2,1)} fusion(bf16[1792,2560]{1,0:T(8,128)(2,1)} %get-tuple-element.406, bf16[2560,1792]{1,0:T(8,128)(2,1)} %get-tuple-element.405, f32[64,1792]{1,0:T(8,128)S(1)} %fusion.126, bf16[64,2560]{1,0:T(8,128)(2,1)S(1)} %all_gather.35, f32[2560]{0:T(1024)S(1)} %get-tuple-element.403, ...), kind=kOutput, calls=%fused_computation.clone.1 | convolution fusion | flops 1175912448 | bytes 19474688 | tf_op jit(solution)/shard_map/while/body/eval_jaxpr/dot_general | solution.py:186
  355.1 8.9 reduce-scatter.5.cloned.1.call-done
  369.3 3.9 collective-permute-done
  376.4 5.4 fusion.126
  381.8 10.3 %convolution_convert_fusion.5 = bf16[64,2560]{1,0:T(8,128)(2,1)} fusion(bf16[1792,2560]{1,0:T(8,128)(2,1)} %get-tuple-element.406, bf16[2560,1792]{1,0:T(8,128)(2,1)} %get-tuple-element.405, f32[64,1792]{1,0:T(8,128)S(1)} %fusion.126, bf16[64,2560]{1,0:T(8,128)(2,1)S(1)} %all_gather.35, f32[2560]{0:T(1024)S(1)} %get-tuple-element.403, ...), kind=kOutput, calls=%fused_computation.clone.1 | convolution fusion | flops 1175912448 | bytes 19474688 | tf_op jit(solution)/shard_map/while/body/eval_jaxpr/dot_general | solution.py:186
  393.0 8.9 reduce-scatter.5.cloned.1.call-done
  407.2 3.9 collective-permute-done
  414.3 5.4 fusion.126
  419.7 10.3 %convolution_convert_fusion.5 = bf16[64,2560]{1,0:T(8,128)(2,1)} fusion(bf16[1792,2560]{1,0:T(8,128)(2,1)} %get-tuple-element.406, bf16[2560,1792]{1,0:T(8,128)(2,1)} %get-tuple-element.405, f32[64,1792]{1,0:T(8,128)S(1)} %fusion.126, bf16[64,2560]{1,0:T(8,128)(2,1)S(1)} %all_gather.35, f32[2560]{0:T(1024)S(1)} %get-tuple-element.403, ...), kind=kOutput, calls=%fused_computation.clone.1 | convolution fusion | flops 1175912448 | bytes 19474688 | tf_op jit(solution)/shard_map/while/body/eval_jaxpr/dot_general | solution.py:186
  430.9 8.9 reduce-scatter.5.cloned.1.call-done
  445.1 3.9 collective-permute-done
  452.2 5.4 fusion.126
  457.5 10.3 %convolution_convert_fusion.5 = bf16[64,2560]{1,0:T(8,128)(2,1)} fusion(bf16[1792,2560]{1,0:T(8,128)(2,1)} %get-tuple-element.406, bf16[2560,1792]{1,0:T(8,128)(2,1)} %get-tuple-element.405, f32[64,1792]{1,0:T(8,128)S(1)} %fusion.126, bf16[64,2560]{1,0:T(8,128)(2,1)S(1)} %all_gather.35, f32[2560]{0:T(1024)S(1)} %get-tuple-element.403, ...), kind=kOutput, calls=%fused_computation.clone.1 | convolution fusion | flops 1175912448 | bytes 19474688 | tf_op jit(solution)/shard_map/while/body/eval_jaxpr/dot_general | solution.py:186
  468.8 8.9 reduce-scatter.5.cloned.1.call-done
  490.0 5.4 fusion.126
  495.4 10.3 %convolution_convert_fusion.5 = bf16[64,2560]{1,0:T(8,128)(2,1)} fusion(bf16[1792,2560]{1,0:T(8,128)(2,1)} %get-tuple-element.406, bf16[2560,1792]{1,0:T(8,128)(2,1)} %get-tuple-element.405, f32[64,1792]{1,0:T(8,128)S(1)} %fusion.126, bf16[64,2560]{1,0:T(8,128)(2,1)S(1)} %all_gather.35, f32[2560]{0:T(1024)S(1)} %get-tuple-element.403, ...), kind=kOutput, calls=%fused_computation.clone.1 | convolution fusion | flops 1175912448 | bytes 19474688 | tf_op jit(solution)/shard_map/while/body/eval_jaxpr/dot_general | solution.py:186
  506.7 8.9 reduce-scatter.5.cloned.1.call-done
  527.9 5.4 fusion.126
  533.3 10.3 %convolution_convert_fusion.5 = bf16[64,2560]{1,0:T(8,128)(2,1)} fusion(bf16[1792,2560]{1,0:T(8,128)(2,1)} %get-tuple-element.406, bf16[2560,1792]{1,0:T(8,128)(2,1)} %get-tuple-element.405, f32[64,1792]{1,0:T(8,128)S(1)} %fusion.126, bf16[64,2560]{1,0:T(8,128)(2,1)S(1)} %all_gather.35, f32[2560]{0:T(1024)S(1)} %get-tuple-element.403, ...), kind=kOutput, calls=%fused_computation.clone.1 | convolution fusion | flops 1175912448 | bytes 19474688 | tf_op jit(solution)/shard_map/while/body/eval_jaxpr/dot_general | solution.py:186
  544.6 8.9 reduce-scatter.5.cloned.1.call-done
  569.8 9.4 %all_gather.31 = bf16[64,1280]{1,0:T(8,128)(2,1)} all-gather(bf16[16,1280]{1,0:T(8,128)(2,1)S(1)} %fusion.57), channel_id=1, replica_groups=mesh['dp'=4,'segment'=4,'mp'=2] {'dp'}, dimensions={0}, use_global_device_ids=true | all-gather | bytes 204800 | tf_op jit(solution)/shard_map/all_gather | solution.py:258
  581.1 4.7 add_convert_fusion.3
  593.6 5.3 fusion.92
  602.5 5.3 fusion.28
  609.4 7.9 multiply_reduce_fusion.8
  622.0 5.0 add_convert_fusion.2
  627.0 7.7 fusion.30
  634.7 9.7 %fusion.45 = f32[64,64,1280]{2,1,0:T(8,128)} fusion(bf16[64,64,256]{2,1,0:T(8,128)(2,1)S(1)} %add_convert_fusion.2, bf16[1280,256]{1,0:T(8,128)(2,1)} %param.26), kind=kOutput, calls=%fused_computation.87 | convolution fusion | flops 2684354560 | bytes 23724032 | tf_op jit(solution)/shard_map/mhc,kc->mhk/dot_general | solution.py:45
  644.5 12.8 %fusion.88 = (f32[64,64,256]{2,1,0:T(8,128)S(1)}, f32[64,64,256]{2,1,0:T(8,128)S(1)}, f32[64,64,256]{2,1,0:T(8,128)}, f32[64,64,256]{2,1,0:T(8,128)}, f32[64,64,256]{2,1,0:T(8,128)}) fusion(f32[64,64,1280]{2,1,0:T(8,128)} %fusion.45), kind=kLoop, calls=%fused_computation.189 | loop fusion | bytes 41943040 | tf_op jit(solution)/shard_map/slice | solution.py:73
  657.4 13.4 %multiply_reduce_fusion = (f32[64,256]{1,0:T(8,128)S(1)}, f32[64,256]{1,0:T(8,128)}, f32[64,256]{1,0:T(8,128)}, f32[64,256]{1,0:T(8,128)S(1)}, f32[64,64,256]{2,1,0:T(8,128)}) fusion(f32[64,256]{1,0:T(8,128)S(1)} %copy.102, f32[64,64,256]{2,1,0:T(8,128)S(1)} %copy-done.2, f32[64,256]{1,0:T(8,128)S(1)} %copy.100, f32[64,256]{1,0:T(8,128)S(1)} %copy-done.12, ...), kind=kLoop, calls=%fused_computation.42 | loop fusion | flops 35586048 | bytes 29818880 | tf_op jit(solution)/shard_map/reduce_sum | solution.py:134
  673.3 8.4 all_gather.33
  696.7 48.8 %all-reduce.21.cloned.1.call-done = bf16[256,512]{1,0:T(8,128)(2,1)} async-done(((bf16[256,512]{1,0:T(8,128)(2,1)}), bf16[256,512]{1,0:T(8,128)(2,1)}) %all-reduce.21.cloned.1.call-update) | async-done | bytes 262160 | tf_op jit(solution)/shard_map/psum | solution.py:254
  746.2 48.3 %all-reduce.19.cloned.1.call-done = bf16[1280,256]{0,1:T(8,128)(2,1)} async-done(((bf16[1280,256]{0,1:T(8,128)(2,1)}), bf16[1280,256]{0,1:T(8,128)(2,1)}) %all-reduce.19.cloned.1.call-update) | async-done | bytes 655376 | tf_op jit(solution)/shard_map/psum | solution.py:18
  796.3 4.8 fusion.37
  801.1 25.4 %all-reduce.8 = (bf16[70,256]{0,1:T(8,128)(2,1)S(1)}, bf16[14,256]{1,0:T(8,128)(2,1)S(1)}, bf16[256,14]{0,1:T(8,128)(2,1)S(1)}, bf16[]{:T(256)}) all-reduce(bf16[70,256]{0,1:T(8,128)(2,1)S(1)} %fusion.37, bf16[14,256]{1,0:T(8,128)(2,1)S(1)} %copy-done.30, ...), channel_id=1, replica_groups=mesh['dp'=4,'segment'=4,'mp'=2] {'dp','mp'}, use_global_device_ids=true, to_apply=%region_28.30 | all-reduce | flops 25089 | bytes 100356 | tf_op jit(solution)/shard_map/psum | solution.py:250
  827.6 25.0 %all-reduce.24 = (bf16[70,256]{0,1:T(8,128)(2,1)S(1)}, bf16[14,256]{1,0:T(8,128)(2,1)S(1)}, bf16[256,14]{0,1:T(8,128)(2,1)S(1)}, bf16[16,1280]{1,0:T(8,128)(2,1)S(1)}, bf16[]{:T(256)}) all-reduce(bf16[70,256]{0,1:T(8,128)(2,1)S(1)} %broadcast_select_fusion.2, ...), channel_id=1, replica_groups=mesh['dp'=4,'segment'=4,'mp'=2] {'segment'}, use_global_device_ids=true, to_apply=%region_29.31 | all-reduce | flops 45569 | bytes 182276 | tf_op jit(solution)/shard_map/psum | solution.py:32
  855.9 35.6 %all-reduce.23.cloned.1.call-done = (bf16[1280,256]{0,1:T(8,128)(2,1)}, bf16[256,512]{1,0:T(8,128)(2,1)}, bf16[1280,512]{1,0:T(8,128)(2,1)}) async-done(((bf16[1280,256]{0,1:T(8,128)(2,1)}, bf16[256,512]{1,0:T(8,128)(2,1)}, bf16[1280,512]{1,0:T(8,128)(2,1)}), (bf16[1280,256]{0,1:T(8,128)(2,1)}, bf16[256,512]{1,0:T(8,128)(2,1)}, bf16[1280,512]{1,0:T(8,128)(2,1)})) %all-reduce.23.cloned.1.call-update) | async-done | bytes 2228240 | tf_op jit(solution)/shard_map/psum | solution.py:32
  (267 shorter events, 144.4 us)
Async XLA Ops:
  7.2 556.9 %copy-start = (bf16[1280,512]{1,0:T(8,128)(2,1)S(1)}, bf16[1280,512]{1,0:T(8,128)(2,1)}, u32[]{:S(2)}) copy-start(bf16[1280,512]{1,0:T(8,128)(2,1)} %param.23) | copy-start | bytes 3932164
  7.2 99.4 %all-gather.4.cloned.1.call-start = ((), (), s32[]{:S(2)}) async-start(), calls=%async_computation.2 | async-start | bytes 11468800 | tf_op jit(solution)/shard_map/all_gather | solution.py:165
  7.9 194.6 %all-gather.6.cloned.1.call-start = ((), (), s32[]{:S(2)}) async-start(), calls=%async_computation.3 | async-start | bytes 11468800 | tf_op jit(solution)/shard_map/all_gather | solution.py:166
  8.7 289.7 %all-gather.8.cloned.1.call-start = ((), (), s32[]{:S(2)}) async-start(), calls=%async_computation.4 | async-start | bytes 11468800 | tf_op jit(solution)/shard_map/all_gather | solution.py:167
  11.2 591.3 %copy-start.4 = (bf16[8,8,64,14]{3,2,1,0:T(8,128)(2,1)}, bf16[8,8,64,14]{3,2,1,0:T(8,128)(2,1)S(1)}, u32[]{:S(2)}) copy-start(bf16[8,8,64,14]{3,2,1,0:T(8,128)(2,1)S(1)} %copy.96) | copy-start | bytes 344068
  14.4 6.5 copy-start.29
  20.8 7.6 copy-start.32
  299.3 26.8 %reduce-scatter.5.cloned.1.call-start = ((), (), s32[]{:S(2)}) async-start(), calls=%async_computation.10 | async-start | bytes 491520 | tf_op jit(solution)/shard_map/while/body/eval_jaxpr/reduce_scatter | solution.py:187
  327.8 7.6 collective-permute-start
  335.3 28.7 %reduce-scatter.5.cloned.1.call-start = ((), (), s32[]{:S(2)}) async-start(), calls=%async_computation.10 | async-start | bytes 491520 | tf_op jit(solution)/shard_map/while/body/eval_jaxpr/reduce_scatter | solution.py:187
  365.7 7.5 collective-permute-start
  373.2 28.7 %reduce-scatter.5.cloned.1.call-start = ((), (), s32[]{:S(2)}) async-start(), calls=%async_computation.10 | async-start | bytes 491520 | tf_op jit(solution)/shard_map/while/body/eval_jaxpr/reduce_scatter | solution.py:187
  403.6 7.5 collective-permute-start
  411.1 28.7 %reduce-scatter.5.cloned.1.call-start = ((), (), s32[]{:S(2)}) async-start(), calls=%async_computation.10 | async-start | bytes 491520 | tf_op jit(solution)/shard_map/while/body/eval_jaxpr/reduce_scatter | solution.py:187
  441.5 7.5 collective-permute-start
  449.0 28.7 %reduce-scatter.5.cloned.1.call-start = ((), (), s32[]{:S(2)}) async-start(), calls=%async_computation.10 | async-start | bytes 491520 | tf_op jit(solution)/shard_map/while/body/eval_jaxpr/reduce_scatter | solution.py:187
  479.4 7.5 collective-permute-start
  486.9 28.7 %reduce-scatter.5.cloned.1.call-start = ((), (), s32[]{:S(2)}) async-start(), calls=%async_computation.10 | async-start | bytes 491520 | tf_op jit(solution)/shard_map/while/body/eval_jaxpr/reduce_scatter | solution.py:187
  517.2 7.5 collective-permute-start
  524.8 28.7 %reduce-scatter.5.cloned.1.call-start = ((), (), s32[]{:S(2)}) async-start(), calls=%async_computation.10 | async-start | bytes 491520 | tf_op jit(solution)/shard_map/while/body/eval_jaxpr/reduce_scatter | solution.py:187
  555.1 7.5 collective-permute-start
  562.7 16.5 %reduce-scatter.3.cloned.1.call-start = ((), (), s32[]{:S(2)}) async-start(), calls=%async_computation.5 | async-start | bytes 24576 | tf_op jit(solution)/shard_map/reduce_scatter | solution.py:218
  564.0 15.9 %copy-start.13 = (f32[16,1280]{1,0:T(8,128)}, f32[16,1280]{1,0:T(8,128)S(1)}, u32[]{:S(2)}) copy-start(f32[16,1280]{1,0:T(8,128)S(1)} %convert_reduce_fusion) | copy-start | bytes 245764
  565.0 128.1 %all-reduce.17.cloned.1.call-start = ((), (), s32[]{:S(2)}) async-start(), calls=%async_computation.6 | async-start | bytes 1310720 | tf_op jit(solution)/shard_map/psum | solution.py:17
  566.0 43.4 %copy-start.35 = (f32[64]{0:T(128)}, f32[64]{0:T(128)S(1)}, u32[]{:S(2)}) copy-start(f32[64]{0:T(128)S(1)} %mul.384) | copy-start | bytes 772
  581.1 6.7 copy-start.11
  599.1 18.5 %copy-start.10 = (f32[64,256]{1,0:T(8,128)}, f32[64,256]{1,0:T(8,128)S(1)}, u32[]{:S(2)}) copy-start(f32[64,256]{1,0:T(8,128)S(1)} %copy.104) | copy-start | bytes 196612
  602.5 6.9 copy-start.24
  602.5 6.9 copy-start.3
  607.8 9.5 %copy-start.7 = (bf16[64,64,256]{2,1,0:T(8,128)(2,1)}, bf16[64,64,256]{2,1,0:T(8,128)(2,1)S(1)}, u32[]{:S(2)}) copy-start(bf16[64,64,256]{2,1,0:T(8,128)(2,1)S(1)} %fusion.28) | copy-start | bytes 6291460
  609.4 7.9 copy-start.8
  644.5 12.9 %copy-start.12 = (f32[64,256]{1,0:T(8,128)S(1)}, f32[64,256]{1,0:T(8,128)}, u32[]{:S(2)}) copy-start(f32[64,256]{1,0:T(8,128)} %copy-done.11) | copy-start | bytes 196612
  644.5 101.0 %all-reduce.21.cloned.1.call-start = ((), (), s32[]{:S(2)}) async-start(), calls=%async_computation.8 | async-start | bytes 524288 | tf_op jit(solution)/shard_map/psum | solution.py:254
  644.5 12.8 %copy-start.2 = (f32[64,64,256]{2,1,0:T(8,128)S(1)}, f32[64,64,256]{2,1,0:T(8,128)}, u32[]{:S(2)}) copy-start(f32[64,64,256]{2,1,0:T(8,128)} %get-tuple-element.299) | copy-start | bytes 12582916
  657.4 25.5 %copy-start.28 = (f32[64,128]{1,0:T(8,128)S(1)}, f32[64,128]{1,0:T(8,128)}, u32[]{:S(2)}) copy-start(f32[64,128]{1,0:T(8,128)} %get-tuple-element.296) | copy-start | bytes 98308
  657.4 27.4 %copy-start.9 = (f32[64,64,14]{1,2,0:T(8,128)S(1)}, f32[64,64,14]{1,2,0:T(8,128)}, u32[]{:S(2)}) copy-start(f32[64,64,14]{1,2,0:T(8,128)} %copy-done.8) | copy-start | bytes 688132
  657.4 27.4 %copy-start.36 = (f32[64]{0:T(128)S(1)}, f32[64]{0:T(128)}, u32[]{:S(2)}) copy-start(f32[64]{0:T(128)} %copy-done.35) | copy-start | bytes 772
  673.3 9.5 %copy-start.26 = (bf16[16,512]{1,0:T(8,128)(2,1)}, bf16[16,512]{1,0:T(8,128)(2,1)S(1)}, u32[]{:S(2)}) copy-start(bf16[16,512]{1,0:T(8,128)(2,1)S(1)} %all_gather.32) | copy-start | bytes 49156
  681.8 8.8 copy-start.25
  682.9 9.2 %copy-start.16 = (f32[64,256]{1,0:T(8,128)}, f32[64,256]{1,0:T(8,128)S(1)}, u32[]{:S(2)}) copy-start(f32[64,256]{1,0:T(8,128)S(1)} %copy.115) | copy-start | bytes 196612
  684.8 7.4 copy-start.23
  687.0 7.2 copy-start.5
  690.5 104.1 %all-reduce.19.cloned.1.call-start = ((), (), s32[]{:S(2)}) async-start(), calls=%async_computation.7 | async-start | bytes 1310720 | tf_op jit(solution)/shard_map/psum | solution.py:18
  693.0 103.3 %copy-start.6 = (bf16[64,64,70]{2,1,0:T(8,128)(2,1)S(1)}, bf16[64,64,70]{2,1,0:T(8,128)(2,1)}, u32[]{:S(2)}) copy-start(bf16[64,64,70]{2,1,0:T(8,128)(2,1)} %concatenate.15) | copy-start | bytes 1720324
  693.1 198.5 %all-reduce.23.cloned.1.call-start = ((), (), s32[]{:S(2)}) async-start(), calls=%async_computation.9 | async-start | bytes 4456448 | tf_op jit(solution)/shard_map/psum | solution.py:32
  696.7 99.5 %copy-start.17 = (f32[64,256]{1,0:T(8,128)S(1)}, f32[64,256]{1,0:T(8,128)}, u32[]{:S(2)}) copy-start(f32[64,256]{1,0:T(8,128)} %copy-done.16) | copy-start | bytes 196612
  796.3 30.9 %copy-start.14 = (f32[16,1280]{1,0:T(8,128)S(1)}, f32[16,1280]{1,0:T(8,128)}, u32[]{:S(2)}) copy-start(f32[16,1280]{1,0:T(8,128)} %copy-done.13) | copy-start | bytes 245764
  796.3 30.9 %copy-start.27 = (bf16[16,512]{1,0:T(8,128)(2,1)S(1)}, bf16[16,512]{1,0:T(8,128)(2,1)}, u32[]{:S(2)}) copy-start(bf16[16,512]{1,0:T(8,128)(2,1)} %copy-done.26) | copy-start | bytes 49156
  (12 other events, 37.5 us)
Sparse Core Ops, SparseCore 0:
  9.9 96.7 all-gather.3
  108.5 94.0 all-gather.5
  204.4 94.0 all-gather.7
  318.3 7.7 reduce-scatter.4
  354.3 9.6 reduce-scatter.4
  392.2 9.6 reduce-scatter.4
  430.1 9.6 reduce-scatter.4
  468.0 9.6 reduce-scatter.4
  505.9 9.6 reduce-scatter.4
  543.8 9.6 reduce-scatter.4
  566.2 9.4 reduce-scatter.2
  644.6 19.7 all-reduce.16
  690.6 54.8 all-reduce.20
  748.4 46.1 all-reduce.18
  797.6 93.9 all-reduce.22
